TPU v7x, 128 devices: a whole 4x4x4 slice. The times are simulated.
128 devices in a mesh: trow: 4 (over x_lo, core), tcol: 4 (over z), visit: 8 (over x_hi, y).
Axes of the slice: x: 4 (x_hi: 2, x_lo: 2; x = x_hi * 2 + x_lo), y: 4, z: 4, core: 2. Of those that a mesh axis runs over, the one named last changes fastest.
Arguments:
- template: float32 [2048, 2048], P(('trow', 'visit'), 'tcol'), may hold values from -6 to 6
- warped: float32 [1536, 256, 256], P(('trow', 'tcol', 'visit')), may hold values from -6 to 6
- coeffs: float32 [1536, 27, 3], P(('trow', 'tcol', 'visit')), may hold values from -2 to 2
- dest_tile: int32 [1536, 1], P(('trow', 'tcol', 'visit')), may hold values from 0 to 15; in each aligned block of 12 rows (0 to 11, 12 to 23, ...) at most 2 rows name the same one
- position: int32 [1536, 1], P(('trow', 'tcol', 'visit')), may hold values from 0 to 3
Outputs:
- difference: float32 [1536, 256, 256], P(('trow', 'tcol', 'visit'))
Inputs may be any that keep to these rules, and one draw needn't show every extreme that they name: `dest_tile`: tile index = tract row times the number of tract columns plus tract column; among the 12 blocks of one device no tile is named more than 2 times. `position`: sub-block row times 512 / 256 plus sub-block column.
All inputs are finite; a program needn't handle non-finite values.
Results may differ from a plain program's by a relative error of at most 0.0003.
Values sent between devices are 32-bit elements; how exact they have to be, the bound alone decides.
No kernel may reach another device: no remote copies, remote signals or barrier semaphores. Data moves between devices by JAX's collectives and lax.ppermute only.
A program may use at most 192 MiB of HBM per device.

v0:
```python
import jax
import jax.numpy as jnp
from jax import lax
from jax.sharding import PartitionSpec as P

BLK = 256
HALF = 10
CAP = 2


SPREADS = (1.0, 2.0, 4.0)
DEGREES = (4, 2, 2)


def extended(block, sides, width):
    for axis, dim in sides:
        count = lax.axis_size(axis)
        forward = [(i, i + 1) for i in range(count - 1)]
        backward = [(target, source) for source, target in forward]
        low = lax.ppermute(
            lax.slice_in_dim(block, block.shape[dim] - width, None, axis=dim), axis, forward
        )
        high = lax.ppermute(lax.slice_in_dim(block, 0, width, axis=dim), axis, backward)
        block = jnp.concatenate([low, block, high], axis=dim)
    return block


def taps_for(spread, power):
    offsets = jnp.arange(-HALF, HALF + 1).astype(jnp.float32)
    weights = jnp.exp(-offsets * offsets / (2.0 * spread * spread))
    for step in range(power):
        weights = weights * offsets
    return weights / jnp.sqrt(jnp.sum(weights * weights))


def band_matrix(tap_weights, length):
    row_ids = jnp.arange(length)[:, None]
    col_ids = jnp.arange(length + 2 * HALF)[None, :]
    offset = col_ids - row_ids
    matrix = jnp.zeros((length, length + 2 * HALF), jnp.float32)
    for tap_index in range(2 * HALF + 1):
        matrix = matrix + jnp.where(offset == tap_index, tap_weights[tap_index], 0.0)
    return matrix


def basis_images(window, out_rows, out_cols):
    highest = lax.Precision.HIGHEST
    stacked = []
    for spread, degree in zip(SPREADS, DEGREES):
        row_passes = [
            jnp.dot(band_matrix(taps_for(spread, power), out_rows), window, precision=highest)
            for power in range(degree + 1)
        ]
        col_bands = [band_matrix(taps_for(spread, power), out_cols) for power in range(degree + 1)]
        for row_power in range(degree + 1):
            for col_power in range(degree + 1 - row_power):
                stacked.append(
                    jnp.dot(row_passes[row_power], col_bands[col_power].T, precision=highest)
                )
    return jnp.stack(stacked)


def block_model(images, coef_block, row_start, col_start):
    zero = jnp.int32(0)
    piece = lax.dynamic_slice(
        images,
        (zero, row_start.astype(jnp.int32), col_start.astype(jnp.int32)),
        (images.shape[0], BLK, BLK),
    )
    mixed = jnp.einsum("bj,bxy->jxy", coef_block, piece, precision=lax.Precision.HIGHEST)
    coords = (jnp.arange(BLK).astype(jnp.float32) - (BLK - 1) / 2.0) / ((BLK - 1) / 2.0)
    return mixed[0] + coords[None, :] * mixed[1] + coords[:, None] * mixed[2]


def on_device(template, warped, coeffs, dest_tile, position):
    highest = lax.Precision.HIGHEST
    strip_rows = template.shape[0]
    tile_cols = template.shape[1]
    row_tiles = lax.axis_size("trow")
    col_tiles = lax.axis_size("tcol")
    tiles = row_tiles * col_tiles
    slots = tiles * CAP
    bases = coeffs.shape[1]
    blocks_here = warped.shape[0]
    target = dest_tile[:, 0]
    block_ids = jnp.arange(blocks_here)
    same_target = target[:, None] == target[None, :]
    before = block_ids[:, None] > block_ids[None, :]
    order = jnp.sum(jnp.where(same_target & before, 1, 0), axis=1).astype(jnp.int32)
    slot_of = target * CAP + order
    slot_hits = jnp.arange(slots)[:, None] == slot_of[None, :]
    placing = slot_hits.astype(jnp.float32)
    send_places = jnp.sum(jnp.where(slot_hits, position[:, 0][None, :], 0), axis=1).reshape(
        (tiles, CAP)
    )
    window = extended(template, ((("trow", "visit"), 0), ("tcol", 1)), HALF)
    strip_images = basis_images(window, strip_rows, tile_cols)
    images = lax.all_gather(strip_images, "visit", axis=1, tiled=True)
    subs = images.shape[1] // BLK
    send_images = jnp.einsum("si,ixy->sxy", placing, warped, precision=highest).reshape(
        (tiles, CAP, BLK, BLK)
    )
    send_coeffs = jnp.einsum("si,ibj->sbj", placing, coeffs, precision=highest).reshape(
        (tiles, CAP, bases, 3)
    )

    def slot_difference(packed):
        image_block, coef_block, sub_place = packed
        model = block_model(images, coef_block, sub_place // subs * BLK, sub_place % subs * BLK)
        return image_block - model

    got_images = lax.all_to_all(
        send_images, ("trow", "tcol"), split_axis=0, concat_axis=0, tiled=True
    )
    got_coeffs = lax.all_to_all(
        send_coeffs, ("trow", "tcol"), split_axis=0, concat_axis=0, tiled=True
    )
    got_places = lax.all_to_all(
        send_places, ("trow", "tcol"), split_axis=0, concat_axis=0, tiled=True
    )
    flat = (
        got_images.reshape((-1, BLK, BLK)),
        got_coeffs.reshape((-1, bases, 3)),
        got_places.reshape((-1,)),
    )
    result = lax.map(slot_difference, flat).reshape(got_images.shape)
    returned = lax.all_to_all(result, ("trow", "tcol"), split_axis=0, concat_axis=0, tiled=True)
    returned = returned.reshape((slots, BLK, BLK))
    return jnp.einsum("si,sxy->ixy", placing, returned, precision=highest)


def solution(mesh):
    return jax.shard_map(
        on_device,
        mesh=mesh,
        in_specs=(
            P(("trow", "visit"), "tcol"),
            P(("trow", "tcol", "visit"), None, None),
            P(("trow", "tcol", "visit"), None, None),
            P(("trow", "tcol", "visit"), None),
            P(("trow", "tcol", "visit"), None),
        ),
        out_specs=P(("trow", "tcol", "visit"), None, None),
        check_vma=False,
    )
```

profile of v0, /device:TPU:1, one launch (start us, length us, event | category | flops | bytes accessed | tf_op | source)
XLA Modules:
  0.0 1726.8 jit_solution(13584206929398370400)
XLA Ops:
  70.7 18.3 %fusion.258 = f32[27,64,512]{2,1,0:T(8,128)} fusion(f32[64,532]{1,0:T(8,128)S(1)} %fusion.808, f32[]{:T(128)} %bitcast.30, f32[]{:T(128)} %bitcast.29, f32[]{:T(128)} %bitcast.28, f32[]{:T(128)} %bitcast.27, f32[]{:T(128)} %bitcast.26, f32[]{:T(128)} %bitcast.25, f32[]{:T(128)} %bitcast.24, f32[]{:T(128)} %bitcast.23, f32[]{:T(128)} %bitcast.22, ...), kind=kOutput, calls=%fused_computation.224 | convolution fusion | flops 226351104 | bytes 267348 | tf_op jit(solution)/shard_map/dot_general | solution.py:58
  102.6 17.9 %fusion.257 = f32[27,64,512]{2,1,0:T(8,128)} fusion(f32[27,64,512]{2,1,0:T(8,128)} %fusion.258, f32[64,532]{1,0:T(8,128)S(1)} %fusion.808, f32[]{:T(128)} %bitcast.52, f32[]{:T(128)} %bitcast.51, f32[]{:T(128)} %bitcast.50, f32[]{:T(128)} %bitcast.49, f32[]{:T(128)} %bitcast.48, f32[]{:T(128)} %bitcast.47, f32[]{:T(128)} %bitcast.46, f32[]{:T(128)} %bitcast.45, ...), kind=kOutput, calls=%fused_computation.222 | convolution fusion | flops 226351104 | bytes 278016 | tf_op jit(solution)/shard_map/dot_general | solution.py:58
  133.9 17.8 %fusion.256 = f32[27,64,512]{2,1,0:T(8,128)} fusion(f32[27,64,512]{2,1,0:T(8,128)} %fusion.257, f32[64,532]{1,0:T(8,128)S(1)} %fusion.808, f32[]{:T(128)} %bitcast.74, f32[]{:T(128)} %bitcast.73, f32[]{:T(128)} %bitcast.72, f32[]{:T(128)} %bitcast.71, f32[]{:T(128)} %bitcast.70, f32[]{:T(128)} %bitcast.69, f32[]{:T(128)} %bitcast.68, f32[]{:T(128)} %bitcast.67, ...), kind=kOutput, calls=%fused_computation.220 | convolution fusion | flops 226351104 | bytes 278016 | tf_op jit(solution)/shard_map/dot_general | solution.py:58
  196.2 17.9 %fusion.220 = f32[27,64,512]{2,1,0:T(8,128)} fusion(f32[27,64,512]{2,1,0:T(8,128)} %fusion.255, f32[64,532]{1,0:T(8,128)S(1)} %fusion.808, f32[]{:T(128)} %bitcast.118, f32[]{:T(128)} %bitcast.117, f32[]{:T(128)} %bitcast.116, f32[]{:T(128)} %bitcast.115, f32[]{:T(128)} %bitcast.114, f32[]{:T(128)} %bitcast.113, f32[]{:T(128)} %bitcast.112, f32[]{:T(128)} %bitcast.111, ...), kind=kOutput, calls=%fused_computation.172 | convolution fusion | flops 226351104 | bytes 278016 | tf_op jit(solution)/shard_map/dot_general | solution.py:58
  214.0 18.0 %fusion.254 = f32[27,64,512]{2,1,0:T(8,128)} fusion(f32[27,64,512]{2,1,0:T(8,128)} %fusion.220, f32[64,532]{1,0:T(8,128)S(1)} %fusion.766, f32[]{:T(128)} %bitcast.30, f32[]{:T(128)} %bitcast.29, f32[]{:T(128)} %bitcast.28, f32[]{:T(128)} %bitcast.27, f32[]{:T(128)} %bitcast.26, f32[]{:T(128)} %bitcast.25, f32[]{:T(128)} %bitcast.24, f32[]{:T(128)} %bitcast.23, ...), kind=kOutput, calls=%fused_computation.216 | convolution fusion | flops 226351104 | bytes 278016 | tf_op jit(solution)/shard_map/dot_general | solution.py:58
  232.0 17.9 %fusion.253 = f32[27,64,512]{2,1,0:T(8,128)} fusion(f32[27,64,512]{2,1,0:T(8,128)} %fusion.254, f32[64,532]{1,0:T(8,128)S(1)} %fusion.766, f32[]{:T(128)} %bitcast.52, f32[]{:T(128)} %bitcast.51, f32[]{:T(128)} %bitcast.50, f32[]{:T(128)} %bitcast.49, f32[]{:T(128)} %bitcast.48, f32[]{:T(128)} %bitcast.47, f32[]{:T(128)} %bitcast.46, f32[]{:T(128)} %bitcast.45, ...), kind=kOutput, calls=%fused_computation.214 | convolution fusion | flops 226351104 | bytes 278016 | tf_op jit(solution)/shard_map/dot_general | solution.py:58
  285.4 17.8 %fusion.250 = f32[27,64,512]{2,1,0:T(8,128)} fusion(f32[27,64,512]{2,1,0:T(8,128)} %fusion.251, f32[64,532]{1,0:T(8,128)S(1)} %fusion.724, f32[]{:T(128)} %bitcast.30, f32[]{:T(128)} %bitcast.29, f32[]{:T(128)} %bitcast.28, f32[]{:T(128)} %bitcast.27, f32[]{:T(128)} %bitcast.26, f32[]{:T(128)} %bitcast.25, f32[]{:T(128)} %bitcast.24, f32[]{:T(128)} %bitcast.23, ...), kind=kOutput, calls=%fused_computation.208 | convolution fusion | flops 226351104 | bytes 278016 | tf_op jit(solution)/shard_map/dot_general | solution.py:58
  303.2 18.1 %fusion.249 = f32[27,64,512]{2,1,0:T(8,128)} fusion(f32[27,64,512]{2,1,0:T(8,128)} %fusion.250, f32[64,532]{1,0:T(8,128)S(1)} %fusion.724, f32[]{:T(128)} %bitcast.52, f32[]{:T(128)} %bitcast.51, f32[]{:T(128)} %bitcast.50, f32[]{:T(128)} %bitcast.49, f32[]{:T(128)} %bitcast.48, f32[]{:T(128)} %bitcast.47, f32[]{:T(128)} %bitcast.46, f32[]{:T(128)} %bitcast.45, ...), kind=kOutput, calls=%fused_computation.206 | convolution fusion | flops 226351104 | bytes 278016 | tf_op jit(solution)/shard_map/dot_general | solution.py:58
  339.1 17.8 %fusion.247 = f32[27,64,512]{2,1,0:T(8,128)} fusion(f32[27,64,512]{2,1,0:T(8,128)} %fusion.248, f32[64,532]{1,0:T(8,128)S(1)} %fusion.682, f32[]{:T(128)} %bitcast.30, f32[]{:T(128)} %bitcast.29, f32[]{:T(128)} %bitcast.28, f32[]{:T(128)} %bitcast.27, f32[]{:T(128)} %bitcast.26, f32[]{:T(128)} %bitcast.25, f32[]{:T(128)} %bitcast.24, f32[]{:T(128)} %bitcast.23, ...), kind=kOutput, calls=%fused_computation.202 | convolution fusion | flops 226351104 | bytes 278016 | tf_op jit(solution)/shard_map/dot_general | solution.py:58
  356.8 17.9 %fusion.246 = f32[27,64,512]{2,1,0:T(8,128)} fusion(f32[27,64,512]{2,1,0:T(8,128)} %fusion.247, f32[64,532]{1,0:T(8,128)S(1)} %fusion.682, f32[]{:T(128)} %bitcast.52, f32[]{:T(128)} %bitcast.51, f32[]{:T(128)} %bitcast.50, f32[]{:T(128)} %bitcast.49, f32[]{:T(128)} %bitcast.48, f32[]{:T(128)} %bitcast.47, f32[]{:T(128)} %bitcast.46, f32[]{:T(128)} %bitcast.45, ...), kind=kOutput, calls=%fused_computation.200 | convolution fusion | flops 226351104 | bytes 278016 | tf_op jit(solution)/shard_map/dot_general | solution.py:58
  374.8 17.8 %fusion.245 = f32[27,64,512]{2,1,0:T(8,128)} fusion(f32[27,64,512]{2,1,0:T(8,128)} %fusion.246, f32[64,532]{1,0:T(8,128)S(1)} %fusion.640, f32[]{:T(128)} %bitcast.30, f32[]{:T(128)} %bitcast.29, f32[]{:T(128)} %bitcast.28, f32[]{:T(128)} %bitcast.27, f32[]{:T(128)} %bitcast.26, f32[]{:T(128)} %bitcast.25, f32[]{:T(128)} %bitcast.24, f32[]{:T(128)} %bitcast.23, ...), kind=kOutput, calls=%fused_computation.198 | convolution fusion | flops 226351104 | bytes 278016 | tf_op jit(solution)/shard_map/dot_general | solution.py:58
  405.9 18.1 %fusion.244 = f32[27,64,512]{2,1,0:T(8,128)} fusion(f32[27,64,512]{2,1,0:T(8,128)} %fusion.245, f32[64,532]{1,0:T(8,128)S(1)} %fusion.598, f32[]{:T(128)} %bitcast.150, f32[]{:T(128)} %bitcast.149, f32[]{:T(128)} %bitcast.148, f32[]{:T(128)} %bitcast.147, f32[]{:T(128)} %bitcast.146, f32[]{:T(128)} %bitcast.145, f32[]{:T(128)} %bitcast.144, f32[]{:T(128)} %bitcast.143, ...), kind=kOutput, calls=%fused_computation.196 | convolution fusion | flops 226351104 | bytes 278016 | tf_op jit(solution)/shard_map/dot_general | solution.py:58
  437.6 17.9 %fusion.243 = f32[27,64,512]{2,1,0:T(8,128)} fusion(f32[27,64,512]{2,1,0:T(8,128)} %fusion.244, f32[64,532]{1,0:T(8,128)S(1)} %fusion.598, f32[]{:T(128)} %bitcast.172, f32[]{:T(128)} %bitcast.171, f32[]{:T(128)} %bitcast.170, f32[]{:T(128)} %bitcast.169, f32[]{:T(128)} %bitcast.168, f32[]{:T(128)} %bitcast.167, f32[]{:T(128)} %bitcast.166, f32[]{:T(128)} %bitcast.165, ...), kind=kOutput, calls=%fused_computation.194 | convolution fusion | flops 226351104 | bytes 278016 | tf_op jit(solution)/shard_map/dot_general | solution.py:58
  504.1 17.9 %fusion.241 = f32[27,64,512]{2,1,0:T(8,128)} fusion(f32[27,64,512]{2,1,0:T(8,128)} %fusion.242, f32[64,532]{1,0:T(8,128)S(1)} %fusion.556, f32[]{:T(128)} %bitcast.172, f32[]{:T(128)} %bitcast.171, f32[]{:T(128)} %bitcast.170, f32[]{:T(128)} %bitcast.169, f32[]{:T(128)} %bitcast.168, f32[]{:T(128)} %bitcast.167, f32[]{:T(128)} %bitcast.166, f32[]{:T(128)} %bitcast.165, ...), kind=kOutput, calls=%fused_computation.190 | convolution fusion | flops 226351104 | bytes 278016 | tf_op jit(solution)/shard_map/dot_general | solution.py:58
  522.0 17.9 %fusion.240 = f32[27,64,512]{2,1,0:T(8,128)} fusion(f32[27,64,512]{2,1,0:T(8,128)} %fusion.241, f32[64,532]{1,0:T(8,128)S(1)} %fusion.514, f32[]{:T(128)} %bitcast.150, f32[]{:T(128)} %bitcast.149, f32[]{:T(128)} %bitcast.148, f32[]{:T(128)} %bitcast.147, f32[]{:T(128)} %bitcast.146, f32[]{:T(128)} %bitcast.145, f32[]{:T(128)} %bitcast.144, f32[]{:T(128)} %bitcast.143, ...), kind=kOutput, calls=%fused_computation.188 | convolution fusion | flops 226351104 | bytes 278016 | tf_op jit(solution)/shard_map/dot_general | solution.py:58
  553.5 17.9 %fusion.239 = f32[27,64,512]{2,1,0:T(8,128)} fusion(f32[27,64,512]{2,1,0:T(8,128)} %fusion.240, f32[64,532]{1,0:T(8,128)S(1)} %fusion.472, f32[]{:T(128)} %bitcast.219, f32[]{:T(128)} %bitcast.218, f32[]{:T(128)} %bitcast.217, f32[]{:T(128)} %bitcast.216, f32[]{:T(128)} %bitcast.215, f32[]{:T(128)} %bitcast.214, f32[]{:T(128)} %bitcast.213, f32[]{:T(128)} %bitcast.212, ...), kind=kOutput, calls=%fused_computation.186 | convolution fusion | flops 226351104 | bytes 278016 | tf_op jit(solution)/shard_map/dot_general | solution.py:58
  615.9 18.0 %fusion.232 = f32[27,64,512]{2,1,0:T(8,128)} fusion(f32[27,64,512]{2,1,0:T(8,128)} %fusion.238, f32[64,532]{1,0:T(8,128)S(1)} %fusion.472, f32[]{:T(128)} %bitcast.263, f32[]{:T(128)} %bitcast.262, f32[]{:T(128)} %bitcast.261, f32[]{:T(128)} %bitcast.260, f32[]{:T(128)} %bitcast.259, f32[]{:T(128)} %bitcast.258, f32[]{:T(128)} %bitcast.257, f32[]{:T(128)} %bitcast.256, ...), kind=kOutput, calls=%fused_computation.176 | convolution fusion | flops 226351104 | bytes 278016 | tf_op jit(solution)/shard_map/dot_general | solution.py:58
  633.9 17.9 %fusion.237 = f32[27,64,512]{2,1,0:T(8,128)} fusion(f32[27,64,512]{2,1,0:T(8,128)} %fusion.232, f32[64,532]{1,0:T(8,128)S(1)} %fusion.430, f32[]{:T(128)} %bitcast.219, f32[]{:T(128)} %bitcast.218, f32[]{:T(128)} %bitcast.217, f32[]{:T(128)} %bitcast.216, f32[]{:T(128)} %bitcast.215, f32[]{:T(128)} %bitcast.214, f32[]{:T(128)} %bitcast.213, f32[]{:T(128)} %bitcast.212, ...), kind=kOutput, calls=%fused_computation.182 | convolution fusion | flops 226351104 | bytes 278016 | tf_op jit(solution)/shard_map/dot_general | solution.py:58
  651.8 17.8 %fusion.236 = f32[27,64,512]{2,1,0:T(8,128)} fusion(f32[27,64,512]{2,1,0:T(8,128)} %fusion.237, f32[64,532]{1,0:T(8,128)S(1)} %fusion.430, f32[]{:T(128)} %bitcast.241, f32[]{:T(128)} %bitcast.240, f32[]{:T(128)} %bitcast.239, f32[]{:T(128)} %bitcast.238, f32[]{:T(128)} %bitcast.237, f32[]{:T(128)} %bitcast.236, f32[]{:T(128)} %bitcast.235, f32[]{:T(128)} %bitcast.234, ...), kind=kOutput, calls=%fused_computation.180 | convolution fusion | flops 226351104 | bytes 278016 | tf_op jit(solution)/shard_map/dot_general | solution.py:58
  669.6 17.9 %fusion.235 = f32[27,64,512]{2,1,0:T(8,128)} fusion(f32[27,64,512]{2,1,0:T(8,128)} %fusion.236, f32[64,532]{1,0:T(8,128)S(1)} %fusion.388, f32[]{:T(128)} %bitcast.219, f32[]{:T(128)} %bitcast.218, f32[]{:T(128)} %bitcast.217, f32[]{:T(128)} %bitcast.216, f32[]{:T(128)} %bitcast.215, f32[]{:T(128)} %bitcast.214, f32[]{:T(128)} %bitcast.213, f32[]{:T(128)} %bitcast.212, ...), kind=kOutput, calls=%fused_computation.178 | convolution fusion | flops 226351104 | bytes 278016 | tf_op jit(solution)/shard_map/dot_general | solution.py:58
  739.6 139.2 %all-to-all-done = f32[16,2,256,256]{3,1,2,0:T(2,128)} async-done(((f32[16,2,256,256]{3,1,2,0:T(2,128)}), f32[16,2,256,256]{3,1,2,0:T(2,128)}, u32[]{:S(2)}, u32[]{:S(2)}) %all-to-all-start) | async-done | bytes 8388640 | tf_op jit(solution)/shard_map/all_to_all | solution.py:112
  886.7 140.6 %all-gather.2.cloned.1.call-done = f32[27,512,512]{2,1,0:T(8,128)} async-done(((f32[27,64,512]{2,1,0:T(8,128)}), f32[27,512,512]{2,1,0:T(8,128)}) %all-gather.2.cloned.1.call-update) | async-done | bytes 28311568 | tf_op jit(solution)/shard_map/all_gather | solution.py:98
  1027.3 551.6 %while.12 = (s32[]{:T(128)}, f32[32,256,256]{2,1,0:T(8,128)}, f32[32,256,256]{2,1,0:T(8,128)}, f32[32,27,3]{1,0,2:T(8,128)S(1)}, s32[32]{0:T(128)S(1)}, /*index=...) while((s32[]{:T(128)}, f32[32,256,256]{2,1,0:T(8,128)}, ...), condition=%wide.region_14.15_spmd, body=%wide.region_13.14_spmd.sunk | while | flops 64029468 | bytes 24384372 | solution.py:126
  1593.4 99.7 %all_to_all.24 = f32[16,2,256,256]{3,1,2,0:T(2,128)S(1)} all-to-all(f32[16,2,256,256]{3,1,2,0:T(2,128)S(1)} %copy.49), channel_id=1, replica_groups=mesh['trow'=4,'tcol'=4,'visit'=8] {'trow','tcol'}, dimensions={0} | all-to-all | bytes 16777216 | tf_op jit(solution)/shard_map/all_to_all | solution.py:127
  (368 shorter events, 876.9 us)
Async XLA Ops:
  6.5 698.2 %copy-start = (f32[12,256,256]{2,1,0:T(8,128)S(1)}, f32[12,256,256]{2,1,0:T(8,128)}, u32[]{:S(2)}) copy-start(f32[12,256,256]{2,1,0:T(8,128)} %param.8) | copy-start | bytes 9437188
  6.5 1020.8 %all-gather.2.cloned.1.call-start = ((), (), s32[]{:S(2)}) async-start(), calls=%async_computation.4 | async-start | bytes 31850496 | tf_op jit(solution)/shard_map/all_gather | solution.py:98
  7.5 39.4 %collective-permute-start = (f32[10,512]{1,0:T(8,128)S(1)}, f32[10,512]{1,0:T(8,128)S(1)}, u32[]{:S(2)}, u32[]{:S(2)}) collective-permute-start(f32[10,512]{1,0:T(8,128)S(1)} %get-tuple-element.131), channel_id=1, source_target_pairs={{0,1},{1,2},{2,3},{3,4},{4,5},{5,6},{6,7},{7,32},{32,33},{33,34},{... | collective-permute-start | bytes 61448 | tf_op jit(solution)/shard_map/ppermute | solution.py:20
  11.6 35.2 %collective-permute-start.1 = (f32[10,512]{1,0:T(8,128)S(1)}, f32[10,512]{1,0:T(8,128)S(1)}, u32[]{:S(2)}, u32[]{:S(2)}) collective-permute-start(f32[10,512]{1,0:T(8,128)S(1)} %get-tuple-element.132), channel_id=1, source_target_pairs={{1,0},{2,1},{3,2},{4,3},{5,4},{6,5},{7,6},{32,7},{33,32},{34,33},{... | collective-permute-start | bytes 61448 | tf_op jit(solution)/shard_map/ppermute | solution.py:23
  47.7 5.5 collective-permute-start.2
  51.3 5.0 collective-permute-start.3
  687.6 0.7 copy-start.2
  687.6 0.8 copy-start.3
  687.6 7.8 copy-start.1
  689.2 11.7 all-to-all-start.2
  700.9 29.8 %all-to-all-start.1 = ((f32[16,1,162]{2,1,0:T(1,128)}), f32[16,1,162]{2,1,0:T(1,128)S(1)}, u32[]{:S(2)}, u32[]{:S(2)}) async-start(f32[16,1,162]{2,1,0:T(1,128)} %reshape.81), calls=%async_computation.1 | async-start | bytes 32768 | tf_op jit(solution)/shard_map/all_to_all | solution.py:115
  730.7 148.2 %all-to-all-start = ((f32[16,2,256,256]{3,1,2,0:T(2,128)}), f32[16,2,256,256]{3,1,2,0:T(2,128)}, u32[]{:S(2)}, u32[]{:S(2)}) async-start(f32[16,2,256,256]{3,1,2,0:T(2,128)} %copy.39), calls=%async_computation | async-start | bytes 16777216 | tf_op jit(solution)/shard_map/all_to_all | solution.py:112
Sparse Core Ops, SparseCore 0:
  687.7 339.5 all-gather.1
where the time goes:
time: 1740 us; the launch traced here: 1730 us
  matrix products  894 us (51%)
  waiting for transfers between devices  287 us (16%)
  local copies, waits for them, and re-layouts  270 us (16%)
  blocking collectives  99.7 us (6%)
  loops' own time  90.4 us (5%)
  other arithmetic  31.9 us (2%)
  starting transfers between devices  31.7 us (2%)
  between operations  21.1 us (1%)
    dot_general x27, matrix products, basis_images(): jnp.dot(row_passes[row_power], col_bands[col_power].T, precision=highest)  483 us
    dot_general x32, matrix products, block_model(): jnp.einsum('bj,bxy->jxy', coef_block, piece, precision=lax.Precision.HIGH...  252 us
    dot_general x11, matrix products, basis_images(): jnp.dot(band_matrix(taps_for(spread, power), out_rows), window, precision...  148 us
    all_gather x1, waiting for transfers between devices, on_device(): images = lax.all_gather(strip_images, 'visit', axis=1, tiled=True)  141 us
    all_to_all x1, waiting for transfers between devices, on_device(): lax.all_to_all(send_images, ('trow', 'tcol'), split_axis=0, concat_axis=0...  139 us
    dynamic_slice x32, local copies, waits for them, and re-layouts, block_model(): lax.dynamic_slice(images, (zero, row_start.astype(jnp.int32), col_start.a...  112 us
    all_to_all x1, blocking collectives, on_device(): lax.all_to_all(result, ('trow', 'tcol'), split_axis=0, concat_axis=0, til...  99.7 us
    another operation x1, loops' own time, on_device(): result = lax.map(slot_difference, flat).reshape(got_images.shape)  90.4 us
  transfers between devices with their start and end apart: 8, of which 4 were waited for; matrix products, arithmetic and copies ran while one was open for 3% of the time, Pallas kernels for 0%

commit v1 on v0

v1 whole, which is shorter than its diff:
```python
import functools

import jax
import jax.numpy as jnp
import numpy as np
from jax import lax
from jax.experimental import pallas as pl
from jax.experimental.pallas import tpu as pltpu
from jax.sharding import PartitionSpec as P

BLK = 256
TILE = 512
HALF = 10
SPREADS = (1.0, 2.0, 4.0)
DEGREES = (4, 2, 2)
FILTERS = [(s, k) for s, d in enumerate(DEGREES) for k in range(d + 1)]
NF = len(FILTERS)
BASIS = {}
for _s, _d in enumerate(DEGREES):
    for _i in range(_d + 1):
        for _j in range(_d + 1 - _i):
            BASIS[(_s, _i, _j)] = len(BASIS)
MAXI = max(DEGREES) + 1

M = 32
CH = 64
NT = BLK // M
KK = NF * CH
WR = 288
WC = 512
ROFF = 16 - HALF
COFF = 128 - HALF


def taps_for(spread, power):
    offsets = np.arange(-HALF, HALF + 1).astype(np.float32)
    weights = np.exp(-offsets * offsets / np.float32(2.0 * spread * spread)).astype(np.float32)
    for _ in range(power):
        weights = weights * offsets
    return (weights / np.sqrt(np.sum(weights * weights))).astype(np.float32)


def column_filters():
    out = np.zeros((256, NF, 128), np.float32)
    for f, (s, k) in enumerate(FILTERS):
        taps = taps_for(SPREADS[s], k)
        for y in range(128):
            out[y : y + 21, f, y] = taps
    return out.reshape(256, NF * 128)


def row_filters():
    out = np.zeros((MAXI, M, NF, CH), np.float32)
    for f, (s, k) in enumerate(FILTERS):
        for i in range(DEGREES[s] + 1 - k):
            taps = taps_for(SPREADS[s], i)
            for x in range(M):
                out[i, x, f, x + ROFF : x + ROFF + 21] = taps
    return out.reshape(MAXI, M, KK)


def split(value):
    high = value.astype(jnp.bfloat16)
    low = (value - high.astype(jnp.float32)).astype(jnp.bfloat16)
    return high, low


def mix_kernel(coef_ref, rows_ref, out_ref):
    def mixed(g):
        total = coef_ref[0, g, 0:1, :] * rows_ref[0]
        for i in range(1, MAXI):
            total = total + coef_ref[0, g, i : i + 1, :] * rows_ref[i]
        return total

    const, across, down = mixed(0), mixed(1), mixed(2)
    across_h, across_l = split(across)
    half = (BLK - 1) / 2.0
    for t in range(NT):
        row = lax.broadcasted_iota(jnp.int32, (M, 1), 0) + t * M
        weight = (row.astype(jnp.float32) - half) * (1.0 / half)
        high, low = split(const + weight * down)
        out_ref[0, t, 0:M, :] = high
        out_ref[0, t, M : 2 * M, :] = across_h
        out_ref[0, t, 2 * M : 3 * M, :] = low
        out_ref[0, t, 3 * M : 4 * M, :] = across_l


def mix_rows(coeffs):
    nb = coeffs.shape[0]
    index = np.zeros((MAXI, NF), np.int32)
    valid = np.zeros((MAXI, NF), np.float32)
    for f, (s, k) in enumerate(FILTERS):
        for i in range(DEGREES[s] + 1 - k):
            index[i, f] = BASIS[(s, i, k)]
            valid[i, f] = 1.0
    picked = jnp.stack(
        [jnp.stack([coeffs[:, int(index[i, f]), :] * float(valid[i, f]) for f in range(NF)], 1) for i in range(MAXI)], 1
    )
    lanes = jnp.repeat(jnp.transpose(picked, (0, 3, 1, 2)), CH, axis=3)
    return pl.pallas_call(
        mix_kernel,
        grid=(nb,),
        in_specs=[
            pl.BlockSpec((1, 3, MAXI, KK), lambda b: (b, 0, 0, 0)),
            pl.BlockSpec((MAXI, M, KK), lambda b: (0, 0, 0)),
        ],
        out_specs=pl.BlockSpec((1, NT, 4 * M, KK), lambda b: (b, 0, 0, 0)),
        out_shape=jax.ShapeDtypeStruct((nb, NT, 4 * M, KK), jnp.bfloat16),
        name="mix_rows",
        cost_estimate=pl.CostEstimate(flops=10**8, bytes_accessed=2 * 10**7, transcendentals=0),
    )(lanes, jnp.asarray(row_filters()))


def window_copies(n, tile_ref, pos_ref, image, window, sem, slot):
    tile, pos = tile_ref[n], pos_ref[n]
    r, c = tile // 4, tile % 4
    pr, pc = pos // 2, pos % 2
    rn = jnp.clip(r + 2 * pr - 1, 0, 3)
    cn = jnp.clip(c + 2 * pc - 1, 0, 3)
    rows = ((r, pl.multiple_of(pr * 240, 8), pl.multiple_of((1 - pr) * 16, 8), 272),
            (rn, pl.multiple_of((1 - pr) * 496, 8), pl.multiple_of(pr * 272, 8), 16))
    cols = ((c, pl.multiple_of(pc * 128, 128), pl.multiple_of((1 - pc) * 128, 128), 384),
            (cn, pl.multiple_of((1 - pc) * 384, 128), pl.multiple_of(pc * 384, 128), 128))
    out = []
    for a, (tr, src_r, dst_r, nr) in enumerate(rows):
        for b, (tc, src_c, dst_c, nc) in enumerate(cols):
            out.append(
                pltpu.make_async_copy(
                    image.at[tr * 4 + tc, pl.ds(src_r, nr), pl.ds(src_c, nc)],
                    window.at[slot, pl.ds(dst_r, nr), pl.ds(dst_c, nc)],
                    sem.at[slot, 2 * a + b],
                )
            )
    return out


def model_kernel(tile_ref, pos_ref, image, warped_ref, rows_ref, cols_ref, out_ref, window, vh, vl, sem):
    n = pl.program_id(0)
    count = pl.num_programs(0)
    slot = n % 2

    @pl.when(n == 0)
    def _():
        for copy in window_copies(n, tile_ref, pos_ref, image, window, sem, slot):
            copy.start()

    @pl.when(n + 1 < count)
    def _():
        for copy in window_copies(n + 1, tile_ref, pos_ref, image, window, sem, 1 - slot):
            copy.start()

    for copy in window_copies(n, tile_ref, pos_ref, image, window, sem, slot):
        copy.wait()

    tile, pos = tile_ref[n], pos_ref[n]
    r, c = tile // 4, tile % 4
    pr, pc = pos // 2, pos % 2

    @pl.when((r == 0) & (pr == 0))
    def _():
        window[slot, 0:16, :] = jnp.zeros((16, WC), jnp.float32)

    @pl.when((r == 3) & (pr == 1))
    def _():
        window[slot, 272:288, :] = jnp.zeros((16, WC), jnp.float32)

    @pl.when((c == 0) & (pc == 0))
    def _():
        window[slot, :, 0:128] = jnp.zeros((WR, 128), jnp.float32)

    @pl.when((c == 3) & (pc == 1))
    def _():
        window[slot, :, 384:512] = jnp.zeros((WR, 128), jnp.float32)

    rolled = pltpu.roll(window[slot], WC - COFF, axis=1)[:, 0:384]
    th, tl = split(rolled)
    for half in range(2):
        lhs = jnp.concatenate(
            [th[:, 128 * half : 128 * half + 256], tl[:, 128 * half : 128 * half + 256], th[:, 128 * half : 128 * half + 256]],
            axis=1,
        )
        for f in range(0, NF, 2):
            width = min(2, NF - f)
            value = jnp.dot(lhs, cols_ref[:, 128 * f : 128 * (f + width)], preferred_element_type=jnp.float32)
            for w in range(width):
                high, low = split(value[:, 128 * w : 128 * (w + 1)])
                vh[f + w, :, 128 * half : 128 * (half + 1)] = high
                vl[f + w, :, 128 * half : 128 * (half + 1)] = low

    mid = (BLK - 1) / 2.0
    across = (lax.broadcasted_iota(jnp.int32, (1, BLK), 1).astype(jnp.float32) - mid) * (1.0 / mid)

    def step(t, carry):
        start = pl.multiple_of(t * M, M)
        wh = vh[:, pl.ds(start, CH), :].reshape(KK, BLK)
        wl = vl[:, pl.ds(start, CH), :].reshape(KK, BLK)
        first = jnp.dot(rows_ref[0, t], wh, preferred_element_type=jnp.float32)
        second = jnp.dot(rows_ref[0, t, 0 : 2 * M, :], wl, preferred_element_type=jnp.float32)
        flat = first[0:M] + first[2 * M : 3 * M] + second[0:M]
        slope = first[M : 2 * M] + first[3 * M : 4 * M] + second[M : 2 * M]
        out_ref[0, pl.ds(start, M), :] = warped_ref[0, pl.ds(start, M), :] - (flat + across * slope)
        return carry

    lax.fori_loop(0, NT, step, 0)


def difference(images, warped, rows, tile, pos):
    nb = warped.shape[0]
    cols = jnp.asarray(column_filters())
    ch, cl = split(cols)
    consts = jnp.concatenate([ch, ch, cl], axis=0)
    spec = pltpu.PrefetchScalarGridSpec(
        num_scalar_prefetch=2,
        grid=(nb,),
        in_specs=[
            pl.BlockSpec(memory_space=pl.ANY),
            pl.BlockSpec((1, BLK, BLK), lambda b, *_: (b, 0, 0)),
            pl.BlockSpec((1, NT, 4 * M, KK), lambda b, *_: (b, 0, 0, 0)),
            pl.BlockSpec((768, NF * 128), lambda b, *_: (0, 0)),
        ],
        out_specs=pl.BlockSpec((1, BLK, BLK), lambda b, *_: (b, 0, 0)),
        scratch_shapes=[
            pltpu.VMEM((2, WR, WC), jnp.float32),
            pltpu.VMEM((NF, WR, BLK), jnp.bfloat16),
            pltpu.VMEM((NF, WR, BLK), jnp.bfloat16),
            pltpu.SemaphoreType.DMA((2, 4)),
        ],
    )
    return pl.pallas_call(
        model_kernel,
        grid_spec=spec,
        out_shape=jax.ShapeDtypeStruct((nb, BLK, BLK), jnp.float32),
        name="difference",
    )(tile, pos, images, warped, rows, consts)


def on_device(template, warped, coeffs, dest_tile, position):
    tile = lax.all_gather(template, "visit", axis=0, tiled=True)
    images = lax.all_gather(tile, ("trow", "tcol"), axis=0)
    rows = mix_rows(coeffs)
    return difference(images, warped, rows, dest_tile[:, 0], position[:, 0])


def solution(mesh):
    return jax.shard_map(
        on_device,
        mesh=mesh,
        in_specs=(
            P(("trow", "visit"), "tcol"),
            P(("trow", "tcol", "visit"), None, None),
            P(("trow", "tcol", "visit"), None, None),
            P(("trow", "tcol", "visit"), None),
            P(("trow", "tcol", "visit"), None),
        ),
        out_specs=P(("trow", "tcol", "visit"), None, None),
        check_vma=False,
    )
```

time: 1740 us -> 215 us (0.12)
  matrix products: 894 us -> 0 us
  local copies, waits for them, and re-layouts: 270 us -> 5.69 us
  waiting for transfers between devices: 287 us -> 131 us
  blocking collectives: 99.7 us -> 0 us
  loops' own time: 90.4 us -> 0 us
  Pallas kernels: 0 us -> 62.2 us
  starting transfers between devices: 31.7 us -> 0.04 us
  other arithmetic: 31.9 us -> 1.82 us
    dot_general x73 -> x0, matrix products: 894 us -> none  [the longest x27 483 us: basis_images(): jnp.dot(row_passes[row_power], col_bands[col_power].T, precision=highest)]
    dynamic_slice x128 -> x0, local copies, waits for them, and re-layouts: 165 us -> none  [the longest x32 112 us: block_model(): lax.dynamic_slice(images, (zero, row_start.astype(jnp.int32), col_start.a...]
    all_to_all x3 -> x0, waiting for transfers between devices: 144 us -> none  [the longest x1 139 us: on_device(): lax.all_to_all(send_images, ('trow', 'tcol'), split_axis=0, concat_axis=0...]
    all_to_all x1 -> x0, blocking collectives: 99.7 us -> none  [on_device(): lax.all_to_all(result, ('trow', 'tcol'), split_axis=0, concat_axis=0, til...]
    another operation x1 -> x0, loops' own time: 90.4 us -> none  [on_device(): result = lax.map(slot_difference, flat).reshape(got_images.shape)]
    pallas_call x0 -> x2, Pallas kernels: none -> 62.2 us  [the longest x1 50.8 us: difference(): pl.pallas_call(model_kernel, grid_spec=spec, out_shape=jax.ShapeDtypeStru...]
    reshape x6 -> x2, local copies, waits for them, and re-layouts: 44.3 us -> 1.63 us  [mix_rows(): lanes = jnp.repeat(jnp.transpose(picked, (0, 3, 1, 2)), CH, axis=3)]
    dynamic_update_slice x32 -> x0, local copies, waits for them, and re-layouts: 23.2 us -> none  [on_device(): result = lax.map(slot_difference, flat).reshape(got_images.shape)]
  transfers between devices with their start and end apart: 8 -> 2, of which waited for: 4 -> 2; matrix products, arithmetic and copies ran while one was open for 3% -> 4% of each run, Pallas kernels for 0% -> 5%
where the time goes in v1:
time: 215 us; the launch traced here: 214 us
  waiting for transfers between devices  131 us (61%)
  Pallas kernels  62.2 us (29%)
  between operations  13.5 us (6%)
  local copies, waits for them, and re-layouts  5.69 us (3%)
    all_gather x1, waiting for transfers between devices, on_device(): images = lax.all_gather(tile, ('trow', 'tcol'), axis=0)  79.7 us
    pallas_call x1, Pallas kernels, difference(): pl.pallas_call(model_kernel, grid_spec=spec, out_shape=jax.ShapeDtypeStru...  50.8 us
    all_gather x1, waiting for transfers between devices, on_device(): tile = lax.all_gather(template, 'visit', axis=0, tiled=True)  50.2 us
    pallas_call x1, Pallas kernels, mix_rows(): pl.pallas_call(mix_kernel, grid=(nb,), in_specs=[pl.BlockSpec((1, 3, MAXI...  11.4 us
  transfers between devices with their start and end apart: 2, of which 2 were waited for; matrix products, arithmetic and copies ran while one was open for 4% of the time, Pallas kernels for 5%

profile of v1, /device:TPU:1, one launch (start us, length us, event | category | flops | bytes accessed | tf_op | source)
XLA Modules:
  0.0 213.9 jit_solution(10960217752129885058)
XLA Ops:
  6.5 0.0 all-gather.4.cloned.1.call-start
  6.5 0.7 all-gather.4.cloned.1.call-update
  7.3 0.0 all-gather.6.cloned.1.call-start
  7.3 50.2 %all-gather.4.cloned.1.call-done = f32[512,512]{1,0:T(8,128)} async-done(((f32[64,512]{1,0:T(8,128)}), f32[512,512]{1,0:T(8,128)}) %all-gather.4.cloned.1.call-update) | async-done | bytes 1048592 | tf_op jit(solution)/shard_map/all_gather | solution.py:238
  57.6 0.0 all-gather.6.cloned.1.call-update
  57.6 0.8 slice.35
  58.4 0.9 fusion.2
  59.3 1.0 fusion.1
  60.3 0.2 stack.32
  60.6 0.2 stack.34
  60.8 0.2 stack.28
  61.0 0.9 fusion.3
  61.9 0.2 stack.30
  62.2 0.8 fusion
  63.1 0.4 broadcast_in_dim.3
  63.5 0.4 reshape.3
  63.9 1.3 copy.10.coef_ref
  65.2 11.4 %mix_rows.1.rows_ref = bf16[12,8,128,704]{3,2,1,0:T(8,128)(2,1)} custom-call(f32[12,3,5,704]{3,2,1,0:T(8,128)} %copy.10.coef_ref, f32[5,32,704]{2,1,0:T(8,128)} %constant.6.clone.rows_ref), custom_call_target="tpu_custom_call" | custom-call | flops 100000000 | bytes 20000000 | tf_op jit(solution)/shard_map/mix_rows/pallas_call | solution.py:100
  76.6 79.7 %all-gather.6.cloned.1.call-done = f32[8192,512]{1,0:T(8,128)} async-done(((f32[512,512]{1,0:T(8,128)}), f32[8192,512]{1,0:T(8,128)}) %all-gather.6.cloned.1.call-update) | async-done | bytes 16777232 | tf_op jit(solution)/shard_map/all_gather | solution.py:239
  156.3 50.8 %difference.1 = f32[12,256,256]{2,1,0:T(8,128)} custom-call(s32[12]{0:T(128)} %bitcast.22, s32[12]{0:T(128)} %bitcast.23, f32[16,512,512]{2,1,0:T(8,128)} %bitcast.19, f32[12,256,256]{2,1,0:T(8,128)} %warped_ref.1, bf16[12,8,128,704]{3,2,1,0:T(8,128)(2,1)} %mix_rows.1.rows_ref, bf16[768,1408]{1,0:T(8,128)(2,1)} %constant.16.cols_ref), custom_call_target="tpu_custom_call" | custom-call | tf_op jit(solution)/shard_map/difference/pallas_call | solution.py:229
  (5 shorter events, 0.1 us)
Async XLA Ops:
  6.5 51.0 %all-gather.4.cloned.1.call-start = ((), (), s32[]{:S(2)}) async-start(), calls=%async_computation | async-start | bytes 1179648 | tf_op jit(solution)/shard_map/all_gather | solution.py:238
  7.3 149.0 %all-gather.6.cloned.1.call-start = ((), (), s32[]{:S(2)}) async-start(), calls=%async_computation.1 | async-start | bytes 17825792 | tf_op jit(solution)/shard_map/all_gather | solution.py:239
Sparse Core Ops, SparseCore 0:
  9.7 47.8 all-gather.3
  59.2 97.0 all-gather.5
